TPU v7x, 32 devices: a whole 2x2x4 slice. The times are simulated.
32 devices in a mesh: groups: 1, expert: 16 (over z, y, core), tensor: 2 (over x).
Axes of the slice: x: 2, y: 2, z: 4, core: 2. Of those that a mesh axis runs over, the one named last changes fastest.
Arguments:
- tokens: bfloat16 [2048, 4096], P(('groups', 'expert')), may hold values from -6 to 6
- expert_ids: int32 [2048, 8], P(('groups', 'expert')), may hold values from 0 to 15, all different within a row; in each aligned block of 128 rows (0 to 127, 128 to 255, ...) at most 96 rows name the same one
- route_weights: float32 [2048, 8], P(('groups', 'expert')), may hold values from 0.1 to 1
- gate_w: bfloat16 [16, 4096, 1536], P('expert', None, 'tensor'), may hold values from -0.09375 to 0.09375
- up_w: bfloat16 [16, 4096, 1536], P('expert', None, 'tensor'), may hold values from -0.09375 to 0.09375
- down_w: bfloat16 [16, 1536, 4096], P('expert', 'tensor'), may hold values from -0.15625 to 0.15625
Outputs:
- moe_out: bfloat16 [2048, 4096], P(('groups', 'expert'), 'tensor')
Inputs may be any that keep to these rules, and one draw needn't show every extreme that they name: `expert_ids`: each row names 8 different experts. Among the rows of one device (aligned blocks of 128 rows) no expert is named more than 96 times, a bound that some block reaches.
All inputs are finite; a program needn't handle non-finite values.
Results may differ from a plain program's by a relative error of at most 0.014.
Values may be sent and summed in bfloat16 or wider, within the bound.
A program may use at most 128 MiB of HBM per device.

v0:
```python
import jax
import jax.numpy as jnp
from jax import lax
from jax.sharding import PartitionSpec as P


def shards(tokens, expert_ids, route_weights, gate_w, up_w, down_w):
    tok_rows, width = tokens.shape
    top_count = expert_ids.shape[1]
    local_experts = gate_w.shape[0]
    expert_devices = lax.axis_size("expert")
    experts_all = local_experts * expert_devices
    capacity = min(tok_rows, 3 * tok_rows * top_count // (2 * experts_all))
    flat_ids = expert_ids.reshape(-1)
    onehot = (flat_ids[:, None] == jnp.arange(experts_all, dtype=jnp.int32)[None, :]).astype(
        jnp.int32
    )
    before = jnp.cumsum(onehot, axis=0) - onehot
    slot = jnp.sum(before * onehot, axis=1)
    destination = flat_ids * capacity + slot
    token_index = jnp.arange(tok_rows * top_count, dtype=jnp.int32) // top_count
    source = jnp.zeros((experts_all * capacity,), jnp.int32).at[destination].set(token_index)
    filled = jnp.zeros((experts_all * capacity,), jnp.bool_).at[destination].set(True)
    outgoing = jnp.where(filled[:, None], tokens[source], jnp.zeros((), tokens.dtype))
    outgoing = outgoing.reshape(experts_all, capacity, tokens.shape[1])
    received = lax.all_to_all(outgoing, "expert", split_axis=0, concat_axis=0, tiled=True)
    slots_in = received.shape[1]
    rows = received.reshape(expert_devices, local_experts, slots_in, width)
    rows = rows.transpose(1, 0, 2, 3).reshape(local_experts, expert_devices * slots_in, width)
    gate = jnp.einsum("erd,edf->erf", rows, gate_w, preferred_element_type=jnp.float32)
    up_part = jnp.einsum("erd,edf->erf", rows, up_w, preferred_element_type=jnp.float32)
    hidden = (jax.nn.silu(gate) * up_part).astype(jnp.bfloat16)
    partial_value = jnp.einsum("erf,efd->erd", hidden, down_w, preferred_element_type=jnp.float32)
    summed = lax.psum_scatter(
        partial_value.astype(jnp.bfloat16), "tensor", scatter_dimension=2, tiled=True
    )
    share = summed.shape[2]
    going_back = summed.reshape(local_experts, expert_devices, slots_in, share)
    going_back = going_back.transpose(1, 0, 2, 3).reshape(experts_all, slots_in, share)
    returned = lax.all_to_all(going_back, "expert", split_axis=0, concat_axis=0, tiled=True)
    share_cols = returned.shape[2]
    flat_back = returned.reshape(experts_all * capacity, share_cols)
    picked = flat_back[destination].reshape(tok_rows, top_count, share_cols)
    mixed = jnp.einsum("tk,tkd->td", route_weights, picked.astype(jnp.float32))
    return mixed.astype(jnp.bfloat16)


def solution(mesh):
    in_specs = (
        P(("groups", "expert"), None),
        P(("groups", "expert"), None),
        P(("groups", "expert"), None),
        P("expert", None, "tensor"),
        P("expert", None, "tensor"),
        P("expert", "tensor", None),
    )
    out_specs = P(("groups", "expert"), "tensor")
    return jax.shard_map(shards, mesh=mesh, in_specs=in_specs, out_specs=out_specs, check_vma=False)
```

profile of v0, /device:TPU:13, one launch (start us, length us, event | category | flops | bytes accessed | tf_op | source)
XLA Modules:
  0.0 667.2 jit_solution(3514439401842417183)
XLA Ops:
  6.5 0.0 copy-start
  6.5 0.0 reduce-scatter.2.cloned.1.call-start
  6.5 0.9 copy.10
  7.4 0.1 eq.29
  7.5 0.1 eq.25
  7.6 0.7 broadcast_multiply_fusion
  8.3 4.5 reduce-window.6
  12.8 0.1 slice.12
  12.9 0.1 copy.12
  13.1 0.1 copy.13
  13.1 0.1 broadcast_add_fusion
  13.2 0.1 copy.9
  13.3 0.1 mul.30
  13.5 4.3 scatter_custom_fusion.1
  17.9 4.3 scatter_custom_fusion
  22.2 0.1 broadcast_in_dim.30
  22.3 0.0 copy-done
  22.3 9.5 %gather_fusion = bf16[1536,4096]{1,0:T(8,128)(2,1)} fusion(bf16[128,4096]{1,0:T(8,128)(2,1)S(1)} %copy-done, s32[2048]{0:T(1024)S(1)} %pad_clamp_fusion), kind=kCustom, calls=%fused_computation | custom fusion | bytes 25171968 | tf_op jit(solution)/shard_map/gather | solution.py:24
  31.8 6.4 broadcast_select_fusion
  38.2 0.0 copy-start.3
  38.2 278.6 %all_to_all.10 = bf16[16,96,4096]{2,1,0:T(8,128)(2,1)S(1)} all-to-all(bf16[16,96,4096]{2,1,0:T(8,128)(2,1)S(1)} %broadcast_select_fusion), channel_id=1, replica_groups=mesh['groups'=1,'expert'=16,'tensor'=2] {'expert'}, dimensions={0} | all-to-all | bytes 25165824 | tf_op jit(solution)/shard_map/all_to_all | solution.py:26
  316.8 0.0 copy-done.3
  316.8 0.0 slice-start
  316.8 11.4 %fusion.2 = f32[1536,768]{1,0:T(8,128)} fusion(bf16[1536,4096]{1,0:T(8,128)(2,1)S(1)} %bitcast.49, bf16[1,4096,768]{2,1,0:T(8,128)(2,1)S(1)} %copy-done.3), kind=kOutput, calls=%fused_computation.8 | convolution fusion | flops 9663676416 | bytes 23592960 | tf_op jit(solution)/shard_map/erd,edf->erf/dot_general | solution.py:31
  328.2 0.0 slice-start.1
  328.2 13.5 %multiply_convert_fusion = bf16[1536,768]{1,0:T(8,128)(2,1)S(1)} fusion(f32[1536,768]{1,0:T(8,128)} %fusion.2, bf16[1536,4096]{1,0:T(8,128)(2,1)S(1)} %bitcast.50, bf16[1,4096,768]{2,1,0:T(8,128)(2,1)} %param.9), kind=kOutput, calls=%fused_computation.12 | convolution fusion | flops 9670754304 | bytes 25952256 | tf_op jit(solution)/shard_map/erd,edf->erf/dot_general | solution.py:30
  341.7 0.0 slice-done
  341.7 0.0 slice-done.1
  341.7 12.4 %fusion = bf16[1,1536,4096]{2,1,0:T(8,128)(2,1)} fusion(bf16[1536,768]{1,0:T(8,128)(2,1)S(1)} %multiply_convert_fusion, bf16[1,768,4096]{2,1,0:T(8,128)(2,1)S(1)} %bitcast.60), kind=kOutput, calls=%fused_computation.5 | convolution fusion | flops 9669967872 | bytes 21233664 | tf_op jit(solution)/shard_map/erf,efd->erd/dot_general | solution.py:33
  354.1 0.0 reduce-scatter.2.cloned.1.call-update
  354.1 145.2 %reduce-scatter.2.cloned.1.call-done = bf16[1,1536,2048]{2,1,0:T(8,128)(2,1)} async-done(((bf16[1,1536,4096]{2,1,0:T(8,128)(2,1)}), bf16[1,1536,2048]{2,1,0:T(8,128)(2,1)}) %reduce-scatter.2.cloned.1.call-update) | async-done | bytes 6291472 | tf_op jit(solution)/shard_map/reduce_scatter | solution.py:34
  499.3 0.0 copy-start.2
  499.3 6.7 all-to-all-start.1
  506.0 0.0 copy-done.2
  506.0 0.1 copy.14
  506.1 137.2 %all-to-all-done.1 = bf16[16,96,2048]{2,1,0:T(8,128)(2,1)} async-done(((bf16[16,96,2048]{2,1,0:T(8,128)(2,1)}), bf16[16,96,2048]{2,1,0:T(8,128)(2,1)}, u32[]{:S(2)}, u32[]{:S(2)}) %all-to-all-start.1) | async-done | bytes 6291488 | tf_op jit(solution)/shard_map/all_to_all | solution.py:40
  643.4 0.0 copy-start.1
  643.4 12.5 %gather_fusion.1 = bf16[1024,2048]{1,0:T(8,128)(2,1)} fusion(bf16[1536,2048]{1,0:T(8,128)(2,1)} %bitcast.11, s32[1024]{0:T(1024)S(1)} %broadcast_clamp_fusion), kind=kCustom, calls=%fused_computation.1 | custom fusion | bytes 8392704 | tf_op jit(solution)/shard_map/gather | solution.py:43
  655.9 3.4 fusion.8
  659.3 1.1 copy.19
  660.4 0.0 copy-done.1
  (11 shorter events, 0.1 us)
Async XLA Ops:
  6.5 15.8 %copy-start = (bf16[128,4096]{1,0:T(8,128)(2,1)S(1)}, bf16[128,4096]{1,0:T(8,128)(2,1)}, u32[]{:S(2)}) copy-start(bf16[128,4096]{1,0:T(8,128)(2,1)} %param.6) | copy-start | bytes 3145732
  6.5 492.8 %reduce-scatter.2.cloned.1.call-start = ((), (), s32[]{:S(2)}) async-start(), calls=%async_computation.3 | async-start | bytes 18874368 | tf_op jit(solution)/shard_map/reduce_scatter | solution.py:34
  38.2 278.6 %copy-start.3 = (bf16[1,4096,768]{2,1,0:T(8,128)(2,1)S(1)}, bf16[1,4096,768]{2,1,0:T(8,128)(2,1)}, u32[]{:S(2)}) copy-start(bf16[1,4096,768]{2,1,0:T(8,128)(2,1)} %param.10) | copy-start | bytes 18874372
  316.8 25.0 %slice-start = ((s8[6291456]{0:T(1024)(128)(4,1)}), s8[2097152]{0:T(1024)(128)(4,1)S(1)}, s32[]{:S(2)}) async-start(s8[6291456]{0:T(1024)(128)(4,1)} %bitcast.59), calls=%async_computation.4 | async-start | bytes 4194304
  328.2 13.5 %slice-start.1 = ((s8[6291456]{0:T(1024)(128)(4,1)}), s8[4194304]{0:T(1024)(128)(4,1)S(1)}, s32[]{:S(2)}) async-start(s8[6291456]{0:T(1024)(128)(4,1)} %bitcast.59), calls=%async_computation.5 | async-start | bytes 8388608
  499.3 6.7 copy-start.2
  499.3 144.1 %all-to-all-start.1 = ((bf16[16,96,2048]{2,1,0:T(8,128)(2,1)}), bf16[16,96,2048]{2,1,0:T(8,128)(2,1)}, u32[]{:S(2)}, u32[]{:S(2)}) async-start(bf16[16,96,2048]{2,1,0:T(8,128)(2,1)} %bitcast.51), calls=%async_computation.2 | async-start | bytes 12582912 | tf_op jit(solution)/shard_map/all_to_all | solution.py:40
  643.4 17.0 %copy-start.1 = (bf16[128,4096]{1,0:T(8,128)(2,1)S(1)}, bf16[128,4096]{1,0:T(8,128)(2,1)}, u32[]{:S(2)}) copy-start(bf16[128,4096]{1,0:T(8,128)(2,1)} %param.6) | copy-start | bytes 3145732
Sparse Core Ops, SparseCore 0:
  354.3 145.0 reduce-scatter.1
where the time goes:
time: 668 us; the launch traced here: 667 us
  waiting for transfers between devices  282 us (42%)
  blocking collectives  279 us (42%)
  matrix products  40.7 us (6%)
  local copies, waits for them, and re-layouts  33.6 us (5%)
  between operations  13.5 us (2%)
  other arithmetic  11.7 us (2%)
    all_to_all x1, blocking collectives, shards(): lax.all_to_all(outgoing, 'expert', split_axis=0, concat_axis=0, tiled=True)  279 us
    reduce_scatter x1, waiting for transfers between devices, shards(): lax.psum_scatter(partial_value.astype(jnp.bfloat16), 'tensor', scatter_di...  145 us
    all_to_all x1, waiting for transfers between devices, shards(): lax.all_to_all(going_back, 'expert', split_axis=0, concat_axis=0, tiled=T...  137 us
    dot_general x1, matrix products, shards(): jnp.einsum('erd,edf->erf', rows, gate_w, preferred_element_type=jnp.float32)  13.5 us
  transfers between devices with their start and end apart: 2, of which 2 were waited for; matrix products, arithmetic and copies ran while one was open for 0% of the time, Pallas kernels for 0%

commit v1 on v0

--- a/solution.py
+++ b/solution.py
@@ -2,6 +2,18 @@
 import jax.numpy as jnp
 from jax import lax
 from jax.sharding import PartitionSpec as P
+
+
+def side_close(x_in, dim_i, page):
+    b_now = x_in.shape
+    everything = x_in.reshape(*b_now[:dim_i], page, b_now[dim_i] // page, *b_now[dim_i + 1 :])
+    return jnp.moveaxis(everything, dim_i, 0)
+
+
+def move_the_node(load, array_dim):
+    prior = list(load.shape[1:])
+    prior[array_dim] *= load.shape[0]
+    return jnp.moveaxis(load, 0, array_dim).reshape(prior)
 
 
 def shards(tokens, expert_ids, route_weights, gate_w, up_w, down_w):
@@ -37,7 +49,20 @@
     share = summed.shape[2]
     going_back = summed.reshape(local_experts, expert_devices, slots_in, share)
     going_back = going_back.transpose(1, 0, 2, 3).reshape(experts_all, slots_in, share)
-    returned = lax.all_to_all(going_back, "expert", split_axis=0, concat_axis=0, tiled=True)
+
+    def render_the_rows(frame, axis_name, inp, tile_in):
+        arr_next, r1 = (lax.axis_size(axis_name), lax.axis_index(axis_name))
+        earlier = side_close(frame, inp, arr_next)
+        block_list = [earlier[r1]]
+        for ii in range(1, arr_next):
+            z_new = earlier[r1 ^ ii]
+            block_list.append(
+                lax.ppermute(z_new, axis_name, [(idx, idx ^ ii) for idx in range(arr_next)])
+            )
+        earlier = jnp.stack(block_list)[r1 ^ jnp.arange(arr_next)]
+        return move_the_node(earlier, tile_in)
+
+    returned = render_the_rows(going_back, "expert", 0, tile_in=0)
     share_cols = returned.shape[2]
     flat_back = returned.reshape(experts_all * capacity, share_cols)
     picked = flat_back[destination].reshape(tok_rows, top_count, share_cols)

time: 668 us -> 695 us (1.040)
  local copies, waits for them, and re-layouts: 33.6 us -> 56.6 us
  starting transfers between devices: 6.66 us -> 18.4 us
  waiting for transfers between devices: 282 us -> 273 us
    all_to_all x1 -> x0, waiting for transfers between devices: 137 us -> none  [shards(): lax.all_to_all(going_back, 'expert', split_axis=0, concat_axis=0, tiled=T...]
    ppermute x0 -> x15, waiting for transfers between devices: none -> 128 us  [render_the_rows(): lax.ppermute(z_new, axis_name, [(idx, idx ^ ii) for idx in range(arr_next)])]
    ppermute x0 -> x15, starting transfers between devices: none -> 18.4 us  [render_the_rows(): lax.ppermute(z_new, axis_name, [(idx, idx ^ ii) for idx in range(arr_next)])]
    unnamed x14 -> x28, local copies, waits for them, and re-layouts: 1.04 us -> 12.5 us
  transfers between devices with their start and end apart: 2 -> 16, of which waited for: 2 -> 12; matrix products, arithmetic and copies ran while one was open for 0% -> 2% of each run, Pallas kernels for 0% -> 0%
where the time goes in v1:
time: 695 us; the launch traced here: 693 us
  blocking collectives  279 us (40%)
  waiting for transfers between devices  273 us (39%)
  local copies, waits for them, and re-layouts  56.6 us (8%)
  matrix products  40.8 us (6%)
  starting transfers between devices  18.4 us (3%)
  between operations  13.7 us (2%)
  other arithmetic  11.8 us (2%)
    all_to_all x1, blocking collectives, shards(): lax.all_to_all(outgoing, 'expert', split_axis=0, concat_axis=0, tiled=True)  279 us
    reduce_scatter x1, waiting for transfers between devices, shards(): lax.psum_scatter(partial_value.astype(jnp.bfloat16), 'tensor', scatter_di...  144 us
    ppermute x15, waiting for transfers between devices, render_the_rows(): lax.ppermute(z_new, axis_name, [(idx, idx ^ ii) for idx in range(arr_next)])  128 us
    ppermute x15, starting transfers between devices, render_the_rows(): lax.ppermute(z_new, axis_name, [(idx, idx ^ ii) for idx in range(arr_next)])  18.4 us
  transfers between devices with their start and end apart: 16, of which 12 were waited for; matrix products, arithmetic and copies ran while one was open for 2% of the time, Pallas kernels for 0%

profile of v1, /device:TPU:13, one launch (start us, length us, event | category | flops | bytes accessed | tf_op | source)
XLA Modules:
  0.0 692.6 jit_solution(7763921871035388048)
XLA Ops:
  6.5 0.9 copy.10
  7.4 0.1 eq.29
  7.5 0.1 eq.25
  7.6 0.7 broadcast_multiply_fusion
  8.3 4.5 reduce-window.6
  12.9 0.1 copy.12
  13.2 0.1 copy.9
  13.3 0.1 mul.30
  13.5 4.3 scatter_custom_fusion.1
  17.9 4.3 scatter_custom_fusion
  22.3 9.5 %gather_fusion = bf16[1536,4096]{1,0:T(8,128)(2,1)} fusion(bf16[128,4096]{1,0:T(8,128)(2,1)S(1)} %copy-done, s32[2048]{0:T(1024)S(1)} %pad_clamp_fusion), kind=kCustom, calls=%fused_computation | custom fusion | bytes 25171968 | tf_op jit(solution)/shard_map/gather | solution.py:36
  31.8 6.4 broadcast_select_fusion
  38.2 278.6 %all_to_all.5 = bf16[16,96,4096]{2,1,0:T(8,128)(2,1)S(1)} all-to-all(bf16[16,96,4096]{2,1,0:T(8,128)(2,1)S(1)} %broadcast_select_fusion), channel_id=1, replica_groups=mesh['groups'=1,'expert'=16,'tensor'=2] {'expert'}, dimensions={0} | all-to-all | bytes 25165824 | tf_op jit(solution)/shard_map/all_to_all | solution.py:38
  316.8 11.4 %fusion.2 = f32[1536,768]{1,0:T(8,128)} fusion(bf16[1536,4096]{1,0:T(8,128)(2,1)S(1)} %bitcast.113, bf16[1,4096,768]{2,1,0:T(8,128)(2,1)S(1)} %copy-done.3), kind=kOutput, calls=%fused_computation.9 | convolution fusion | flops 9663676416 | bytes 23592960 | tf_op jit(solution)/shard_map/erd,edf->erf/dot_general | solution.py:43
  328.2 13.5 %multiply_convert_fusion = bf16[1536,768]{1,0:T(8,128)(2,1)S(1)} fusion(f32[1536,768]{1,0:T(8,128)} %fusion.2, bf16[1536,4096]{1,0:T(8,128)(2,1)S(1)} %bitcast.114, bf16[1,4096,768]{2,1,0:T(8,128)(2,1)} %param.9), kind=kOutput, calls=%fused_computation.13 | convolution fusion | flops 9670754304 | bytes 25952256 | tf_op jit(solution)/shard_map/erd,edf->erf/dot_general | solution.py:42
  341.8 12.5 %fusion = bf16[1,1536,4096]{2,1,0:T(8,128)(2,1)} fusion(bf16[1536,768]{1,0:T(8,128)(2,1)S(1)} %multiply_convert_fusion, bf16[1,768,4096]{2,1,0:T(8,128)(2,1)S(1)} %bitcast.124), kind=kOutput, calls=%fused_computation.6 | convolution fusion | flops 9669967872 | bytes 21233664 | tf_op jit(solution)/shard_map/erf,efd->erd/dot_general | solution.py:45
  354.3 0.6 copy-done.2
  354.9 0.1 copy.14
  355.2 144.3 %reduce-scatter.2.cloned.1.call-done = bf16[1,1536,2048]{2,1,0:T(8,128)(2,1)} async-done(((bf16[1,1536,4096]{2,1,0:T(8,128)(2,1)}), bf16[1,1536,2048]{2,1,0:T(8,128)(2,1)}) %reduce-scatter.2.cloned.1.call-update) | async-done | bytes 6291472 | tf_op jit(solution)/shard_map/reduce_scatter | solution.py:46
  499.5 4.4 dynamic-slice_bitcast_fusion
  503.9 0.8 collective-permute-start
  504.7 0.3 collective-permute-start.1
  505.0 1.4 collective-permute-start.2
  506.4 0.3 collective-permute-start.3
  506.7 1.6 collective-permute-start.4
  508.3 0.3 collective-permute-start.5
  508.5 0.8 bitcast_dynamic-update-slice_fusion.14
  509.3 6.1 collective-permute-done.1
  515.4 1.5 collective-permute-start.6
  516.9 0.8 bitcast_dynamic-update-slice_fusion.13
  517.7 6.6 collective-permute-done.2
  524.3 2.1 collective-permute-start.7
  526.5 0.8 bitcast_dynamic-update-slice_fusion.12
  527.3 0.3 collective-permute-start.8
  527.6 0.8 bitcast_dynamic-update-slice_fusion.11
  528.4 2.1 collective-permute-start.9
  530.5 0.8 bitcast_dynamic-update-slice_fusion.10
  531.2 17.3 %collective-permute-done.5 = bf16[1,96,2048]{2,1,0:T(8,128)(2,1)S(1)} collective-permute-done((bf16[1,96,2048]{2,1,0:T(8,128)(2,1)S(1)}, bf16[1,96,2048]{2,1,0:T(8,128)(2,1)S(1)}, u32[]{:S(2)}, u32[]{:S(2)}) %collective-permute-start.5) | collective-permute-done | bytes 393248 | tf_op jit(solution)/shard_map/ppermute | solution.py:60
  548.6 4.7 collective-permute-start.10
  553.3 0.8 bitcast_dynamic-update-slice_fusion.9
  554.0 3.0 collective-permute-done.6
  557.0 0.3 collective-permute-start.11
  557.2 0.8 bitcast_dynamic-update-slice_fusion.8
  558.0 2.5 collective-permute-start.12
  560.5 0.8 bitcast_dynamic-update-slice_fusion.7
  561.3 32.8 %collective-permute-done.8 = bf16[1,96,2048]{2,1,0:T(8,128)(2,1)S(1)} collective-permute-done((bf16[1,96,2048]{2,1,0:T(8,128)(2,1)S(1)}, bf16[1,96,2048]{2,1,0:T(8,128)(2,1)S(1)}, u32[]{:S(2)}, u32[]{:S(2)}) %collective-permute-start.8) | collective-permute-done | bytes 393248 | tf_op jit(solution)/shard_map/ppermute | solution.py:60
  594.1 0.8 bitcast_dynamic-update-slice_fusion.6
  594.8 16.1 %collective-permute-done.9 = bf16[1,96,2048]{2,1,0:T(8,128)(2,1)S(1)} collective-permute-done((bf16[1,96,2048]{2,1,0:T(8,128)(2,1)S(1)}, bf16[1,96,2048]{2,1,0:T(8,128)(2,1)S(1)}, u32[]{:S(2)}, u32[]{:S(2)}) %collective-permute-start.9) | collective-permute-done | bytes 393248 | tf_op jit(solution)/shard_map/ppermute | solution.py:60
  610.9 0.3 collective-permute-start.14
  611.2 0.8 bitcast_dynamic-update-slice_fusion.5
  612.0 15.7 %collective-permute-done.10 = bf16[1,96,2048]{2,1,0:T(8,128)(2,1)S(1)} collective-permute-done((bf16[1,96,2048]{2,1,0:T(8,128)(2,1)S(1)}, bf16[1,96,2048]{2,1,0:T(8,128)(2,1)S(1)}, u32[]{:S(2)}, u32[]{:S(2)}) %collective-permute-start.10) | collective-permute-done | bytes 393248 | tf_op jit(solution)/shard_map/ppermute | solution.py:60
  627.8 0.8 bitcast_dynamic-update-slice_fusion.4
  628.5 7.7 %collective-permute-done.11 = bf16[1,96,2048]{2,1,0:T(8,128)(2,1)S(1)} collective-permute-done((bf16[1,96,2048]{2,1,0:T(8,128)(2,1)S(1)}, bf16[1,96,2048]{2,1,0:T(8,128)(2,1)S(1)}, u32[]{:S(2)}, u32[]{:S(2)}) %collective-permute-start.11) | collective-permute-done | bytes 393248 | tf_op jit(solution)/shard_map/ppermute | solution.py:60
  636.2 0.8 bitcast_dynamic-update-slice_fusion.3
  637.0 8.1 %collective-permute-done.12 = bf16[1,96,2048]{2,1,0:T(8,128)(2,1)S(1)} collective-permute-done((bf16[1,96,2048]{2,1,0:T(8,128)(2,1)S(1)}, bf16[1,96,2048]{2,1,0:T(8,128)(2,1)S(1)}, u32[]{:S(2)}, u32[]{:S(2)}) %collective-permute-start.12) | collective-permute-done | bytes 393248 | tf_op jit(solution)/shard_map/ppermute | solution.py:60
  645.1 0.8 bitcast_dynamic-update-slice_fusion.2
  645.9 7.2 %collective-permute-done.13 = bf16[1,96,2048]{2,1,0:T(8,128)(2,1)S(1)} collective-permute-done((bf16[1,96,2048]{2,1,0:T(8,128)(2,1)S(1)}, bf16[1,96,2048]{2,1,0:T(8,128)(2,1)S(1)}, u32[]{:S(2)}, u32[]{:S(2)}) %collective-permute-start.13) | collective-permute-done | bytes 393248 | tf_op jit(solution)/shard_map/ppermute | solution.py:60
  653.1 0.8 bitcast_dynamic-update-slice_fusion.1
  653.9 7.7 %collective-permute-done.14 = bf16[1,96,2048]{2,1,0:T(8,128)(2,1)S(1)} collective-permute-done((bf16[1,96,2048]{2,1,0:T(8,128)(2,1)S(1)}, bf16[1,96,2048]{2,1,0:T(8,128)(2,1)S(1)}, u32[]{:S(2)}, u32[]{:S(2)}) %collective-permute-start.14) | collective-permute-done | bytes 393248 | tf_op jit(solution)/shard_map/ppermute | solution.py:60
  661.6 0.8 bitcast_dynamic-update-slice_fusion
  662.4 6.4 gather_fusion.1
  668.7 12.5 %gather_fusion.2 = bf16[1024,2048]{1,0:T(8,128)(2,1)} fusion(bf16[1536,2048]{1,0:T(8,128)(2,1)} %bitcast.111, s32[1024]{0:T(1024)S(1)} %broadcast_clamp_fusion), kind=kCustom, calls=%fused_computation.2 | custom fusion | bytes 8392704 | tf_op jit(solution)/shard_map/gather | solution.py:68
  681.2 3.4 fusion.8
  684.7 1.1 copy.19
  (35 shorter events, 0.5 us)
Async XLA Ops:
  6.5 15.8 %copy-start = (bf16[128,4096]{1,0:T(8,128)(2,1)S(1)}, bf16[128,4096]{1,0:T(8,128)(2,1)}, u32[]{:S(2)}) copy-start(bf16[128,4096]{1,0:T(8,128)(2,1)} %param.6) | copy-start | bytes 3145732
  6.5 492.9 %reduce-scatter.2.cloned.1.call-start = ((), (), s32[]{:S(2)}) async-start(), calls=%async_computation.2 | async-start | bytes 18874368 | tf_op jit(solution)/shard_map/reduce_scatter | solution.py:46
  38.2 278.6 %copy-start.3 = (bf16[1,4096,768]{2,1,0:T(8,128)(2,1)S(1)}, bf16[1,4096,768]{2,1,0:T(8,128)(2,1)}, u32[]{:S(2)}) copy-start(bf16[1,4096,768]{2,1,0:T(8,128)(2,1)} %param.10) | copy-start | bytes 18874372
  316.8 25.0 %slice-start = ((s8[6291456]{0:T(1024)(128)(4,1)}), s8[2097152]{0:T(1024)(128)(4,1)S(1)}, s32[]{:S(2)}) async-start(s8[6291456]{0:T(1024)(128)(4,1)} %bitcast.123), calls=%async_computation.3 | async-start | bytes 4194304
  328.2 13.5 %slice-start.1 = ((s8[6291456]{0:T(1024)(128)(4,1)}), s8[4194304]{0:T(1024)(128)(4,1)S(1)}, s32[]{:S(2)}) async-start(s8[6291456]{0:T(1024)(128)(4,1)} %bitcast.123), calls=%async_computation.4 | async-start | bytes 8388608
  354.2 0.7 copy-start.2
  503.9 4.4 collective-permute-start
  504.7 10.7 %collective-permute-start.1 = (bf16[1,96,2048]{2,1,0:T(8,128)(2,1)S(1)}, bf16[1,96,2048]{2,1,0:T(8,128)(2,1)S(1)}, u32[]{:S(2)}, u32[]{:S(2)}) collective-permute-start(bf16[1,96,2048]{2,1,0:T(8,128)(2,1)S(1)} %get-tuple-element.18), channel_id=1, source_target_pairs={{0,4},{2,6},{4,0},{6,2},{8,12},{10,14},{12,8},{14,10},{16,20},{18,... | collective-permute-start | bytes 1179656 | tf_op jit(solution)/shard_map/ppermute | solution.py:60
  505.0 19.3 %collective-permute-start.2 = (bf16[1,96,2048]{2,1,0:T(8,128)(2,1)S(1)}, bf16[1,96,2048]{2,1,0:T(8,128)(2,1)S(1)}, u32[]{:S(2)}, u32[]{:S(2)}) collective-permute-start(bf16[1,96,2048]{2,1,0:T(8,128)(2,1)S(1)} %get-tuple-element.17), channel_id=1, source_target_pairs={{0,6},{2,4},{4,2},{6,0},{8,14},{10,12},{12,10},{14,8},{16,22},{18,... | collective-permute-start | bytes 1179656 | tf_op jit(solution)/shard_map/ppermute | solution.py:60
  506.4 20.9 %collective-permute-start.3 = (bf16[1,96,2048]{2,1,0:T(8,128)(2,1)S(1)}, bf16[1,96,2048]{2,1,0:T(8,128)(2,1)S(1)}, u32[]{:S(2)}, u32[]{:S(2)}) collective-permute-start(bf16[1,96,2048]{2,1,0:T(8,128)(2,1)S(1)} %get-tuple-element.16), channel_id=1, source_target_pairs={{0,8},{2,10},{4,12},{6,14},{8,0},{10,2},{12,4},{14,6},{16,24},{18,... | collective-permute-start | bytes 1179656 | tf_op jit(solution)/shard_map/ppermute | solution.py:60
  506.7 21.7 %collective-permute-start.4 = (bf16[1,96,2048]{2,1,0:T(8,128)(2,1)S(1)}, bf16[1,96,2048]{2,1,0:T(8,128)(2,1)S(1)}, u32[]{:S(2)}, u32[]{:S(2)}) collective-permute-start(bf16[1,96,2048]{2,1,0:T(8,128)(2,1)S(1)} %get-tuple-element.15), channel_id=1, source_target_pairs={{0,10},{2,8},{4,14},{6,12},{8,2},{10,0},{12,6},{14,4},{16,26},{18,... | collective-permute-start | bytes 1179656 | tf_op jit(solution)/shard_map/ppermute | solution.py:60
  508.3 40.3 %collective-permute-start.5 = (bf16[1,96,2048]{2,1,0:T(8,128)(2,1)S(1)}, bf16[1,96,2048]{2,1,0:T(8,128)(2,1)S(1)}, u32[]{:S(2)}, u32[]{:S(2)}) collective-permute-start(bf16[1,96,2048]{2,1,0:T(8,128)(2,1)S(1)} %get-tuple-element.14), channel_id=1, source_target_pairs={{0,12},{2,14},{4,8},{6,10},{8,4},{10,6},{12,0},{14,2},{16,28},{18,... | collective-permute-start | bytes 1179656 | tf_op jit(solution)/shard_map/ppermute | solution.py:60
  515.4 41.6 %collective-permute-start.6 = (bf16[1,96,2048]{2,1,0:T(8,128)(2,1)S(1)}, bf16[1,96,2048]{2,1,0:T(8,128)(2,1)S(1)}, u32[]{:S(2)}, u32[]{:S(2)}) collective-permute-start(bf16[1,96,2048]{2,1,0:T(8,128)(2,1)S(1)} %get-tuple-element.13), channel_id=1, source_target_pairs={{0,14},{2,12},{4,10},{6,8},{8,6},{10,4},{12,2},{14,0},{16,30},{18,... | collective-permute-start | bytes 1179656 | tf_op jit(solution)/shard_map/ppermute | solution.py:60
  524.3 33.7 %collective-permute-start.7 = (bf16[1,96,2048]{2,1,0:T(8,128)(2,1)S(1)}, bf16[1,96,2048]{2,1,0:T(8,128)(2,1)S(1)}, u32[]{:S(2)}, u32[]{:S(2)}) collective-permute-start(bf16[1,96,2048]{2,1,0:T(8,128)(2,1)S(1)} %get-tuple-element.12), channel_id=1, source_target_pairs={{0,16},{2,18},{4,20},{6,22},{8,24},{10,26},{12,28},{14,30},{16,0},... | collective-permute-start | bytes 1179656 | tf_op jit(solution)/shard_map/ppermute | solution.py:60
  527.3 66.8 %collective-permute-start.8 = (bf16[1,96,2048]{2,1,0:T(8,128)(2,1)S(1)}, bf16[1,96,2048]{2,1,0:T(8,128)(2,1)S(1)}, u32[]{:S(2)}, u32[]{:S(2)}) collective-permute-start(bf16[1,96,2048]{2,1,0:T(8,128)(2,1)S(1)} %get-tuple-element.11), channel_id=1, source_target_pairs={{0,18},{2,16},{4,22},{6,20},{8,26},{10,24},{12,30},{14,28},{16,2},... | collective-permute-start | bytes 1179656 | tf_op jit(solution)/shard_map/ppermute | solution.py:60
  528.4 82.6 %collective-permute-start.9 = (bf16[1,96,2048]{2,1,0:T(8,128)(2,1)S(1)}, bf16[1,96,2048]{2,1,0:T(8,128)(2,1)S(1)}, u32[]{:S(2)}, u32[]{:S(2)}) collective-permute-start(bf16[1,96,2048]{2,1,0:T(8,128)(2,1)S(1)} %get-tuple-element.10), channel_id=1, source_target_pairs={{0,20},{2,22},{4,16},{6,18},{8,28},{10,30},{12,24},{14,26},{16,4},... | collective-permute-start | bytes 1179656 | tf_op jit(solution)/shard_map/ppermute | solution.py:60
  548.6 79.2 %collective-permute-start.10 = (bf16[1,96,2048]{2,1,0:T(8,128)(2,1)S(1)}, bf16[1,96,2048]{2,1,0:T(8,128)(2,1)S(1)}, u32[]{:S(2)}, u32[]{:S(2)}) collective-permute-start(bf16[1,96,2048]{2,1,0:T(8,128)(2,1)S(1)} %get-tuple-element.9), channel_id=1, source_target_pairs={{0,22},{2,20},{4,18},{6,16},{8,30},{10,28},{12,26},{14,24},{16,6},... | collective-permute-start | bytes 1179656 | tf_op jit(solution)/shard_map/ppermute | solution.py:60
  557.0 79.2 %collective-permute-start.11 = (bf16[1,96,2048]{2,1,0:T(8,128)(2,1)S(1)}, bf16[1,96,2048]{2,1,0:T(8,128)(2,1)S(1)}, u32[]{:S(2)}, u32[]{:S(2)}) collective-permute-start(bf16[1,96,2048]{2,1,0:T(8,128)(2,1)S(1)} %get-tuple-element.8), channel_id=1, source_target_pairs={{0,24},{2,26},{4,28},{6,30},{8,16},{10,18},{12,20},{14,22},{16,8},... | collective-permute-start | bytes 1179656 | tf_op jit(solution)/shard_map/ppermute | solution.py:60
  558.0 87.1 %collective-permute-start.12 = (bf16[1,96,2048]{2,1,0:T(8,128)(2,1)S(1)}, bf16[1,96,2048]{2,1,0:T(8,128)(2,1)S(1)}, u32[]{:S(2)}, u32[]{:S(2)}) collective-permute-start(bf16[1,96,2048]{2,1,0:T(8,128)(2,1)S(1)} %get-tuple-element.7), channel_id=1, source_target_pairs={{0,26},{2,24},{4,30},{6,28},{8,18},{10,16},{12,22},{14,20},{16,10}... | collective-permute-start | bytes 1179656 | tf_op jit(solution)/shard_map/ppermute | solution.py:60
  594.1 59.0 %collective-permute-start.13 = (bf16[1,96,2048]{2,1,0:T(8,128)(2,1)S(1)}, bf16[1,96,2048]{2,1,0:T(8,128)(2,1)S(1)}, u32[]{:S(2)}, u32[]{:S(2)}) collective-permute-start(bf16[1,96,2048]{2,1,0:T(8,128)(2,1)S(1)} %get-tuple-element.6), channel_id=1, source_target_pairs={{0,28},{2,30},{4,24},{6,26},{8,20},{10,22},{12,16},{14,18},{16,12}... | collective-permute-start | bytes 1179656 | tf_op jit(solution)/shard_map/ppermute | solution.py:60
  610.9 50.7 %collective-permute-start.14 = (bf16[1,96,2048]{2,1,0:T(8,128)(2,1)S(1)}, bf16[1,96,2048]{2,1,0:T(8,128)(2,1)S(1)}, u32[]{:S(2)}, u32[]{:S(2)}) collective-permute-start(bf16[1,96,2048]{2,1,0:T(8,128)(2,1)S(1)} %get-tuple-element.5), channel_id=1, source_target_pairs={{0,30},{2,28},{4,26},{6,24},{8,22},{10,20},{12,18},{14,16},{16,14}... | collective-permute-start | bytes 1179656 | tf_op jit(solution)/shard_map/ppermute | solution.py:60
  668.7 17.0 %copy-start.1 = (bf16[128,4096]{1,0:T(8,128)(2,1)S(1)}, bf16[128,4096]{1,0:T(8,128)(2,1)}, u32[]{:S(2)}) copy-start(bf16[128,4096]{1,0:T(8,128)(2,1)} %param.6) | copy-start | bytes 3145732
Sparse Core Ops, SparseCore 0:
  354.4 145.0 reduce-scatter.1
